TPU v7x, 32 devices: a whole 2x2x4 slice. The times are simulated.
32 devices in a mesh: trial: 2 (over x), freq: 4 (over y, core), lst: 4 (over z).
Axes of the slice: x: 2, y: 2, z: 4, core: 2. Of those that a mesh axis runs over, the one named last changes fastest.
Arguments:
- sky_east: bfloat16 [8192], P(('trial', 'freq')), parts along dimension 0, may hold values from -0.59765625 to 0.59765625
- sky_north: bfloat16 [8192], P(('trial', 'freq')), parts along dimension 0, may hold values from -0.59765625 to 0.59765625
- sky_flux: bfloat16 [8192], P(('trial', 'freq')), parts along dimension 0, may hold values from 0.19921875 to 5
- sky_scint: bfloat16 [8192, 1024], P(('trial', 'freq'), 'lst'), parts along dimension 0, may hold values from 0.19921875 to 1.796875
- visible: int32 [256, 32], P(('trial', 'lst')), parts along dimension 0, may hold values 0 or 1
- antenna_coords: float32 [350, 2], replicated, may hold values from -150 to 150, as said below
- baseline_antennas: int32 [256, 2], replicated, may hold values from 0 to 349, as said below
- filter_taps: bfloat16 [8, 257], P('freq'), may hold values from -0.375 to 0.375
Outputs:
- visibility: bfloat16 [16, 2, 256, 1024], P(('trial', 'freq'), None, None, 'lst'), parts along dimension 0
- filtered: bfloat16 [16, 2, 256, 1024], P(('trial', 'freq'), None, None, 'lst'), parts along dimension 0
There are 2 independent parts, one for each index of `trial`. A program takes and returns all parts, laid end to end along the dimension named above; an argument that names none is the same for every part. Nothing has to cross between parts.
Inputs may be any that keep to these rules, and one draw needn't show every extreme that they name: `baseline_antennas`: each row names two different antennas. `antenna_coords`: positions in metres; no two antennas are closer than 11 metres.
All inputs are finite; a program needn't handle non-finite values. No bound on the sum of `visible` on one device may be relied on, other than what follows from the above.
Results may differ from a plain program's by a relative error of at most 0.0061.
Values may be sent and summed in bfloat16 or wider, within the bound.
A program may use at most 64 MiB of HBM per device.

v0:
```python
import math

import jax
import jax.numpy as jnp
from jax import lax
from jax.sharding import PartitionSpec as P

SRC_BLOCK = 128
TAIL = 256
BLOCK_T = 8


C_LIGHT = 299792458.0
NU_START = 150000000.0
NU_STEP = 97656.25
OMEGA_STEP = 4.37526e-05
BEAM_SIGMA = 0.35
CENTRE_START = -0.045
TWO_PI = 2.0 * math.pi


def shifted(block, axis, distance):
    devices = range(lax.axis_size(axis))
    route = [(i - distance, i) for i in devices if i - distance in devices]
    return lax.ppermute(block, axis, route)


def banded_taps(filter_taps, time_count):
    chan_count = filter_taps.shape[0]
    row_count = TAIL + time_count
    padded_len = TAIL + 2 * time_count
    lead_zeros = jnp.zeros((chan_count, time_count - 1), filter_taps.dtype)
    trail_zeros = jnp.zeros((chan_count, time_count), filter_taps.dtype)
    padded = jnp.concatenate([lead_zeros, filter_taps, trail_zeros], axis=1)
    tiled = jnp.broadcast_to(padded[:, None, :], (chan_count, row_count, padded_len)).reshape(
        chan_count, row_count * padded_len
    )
    skewed = tiled[:, : row_count * (padded_len - 1)].reshape(chan_count, row_count, padded_len - 1)
    return skewed[:, :, row_count - 1 : row_count - 1 + time_count]


def shards(
    sky_east,
    sky_north,
    sky_flux,
    sky_scint,
    visible,
    antenna_coords,
    baseline_antennas,
    filter_taps,
):
    chan_count = filter_taps.shape[0]
    time_count = visible.shape[0] * BLOCK_T
    line_count = baseline_antennas.shape[0]
    total_sources = sky_east.shape[0] * lax.axis_size("freq")
    scale_norm = 1.0 / math.sqrt(total_sources)
    antenna_range = jnp.arange(antenna_coords.shape[0])
    pair_select = (baseline_antennas[:, 0:1] == antenna_range[None, :]).astype(jnp.float32) - (
        baseline_antennas[:, 1:2] == antenna_range[None, :]
    ).astype(jnp.float32)
    baseline_both = jnp.dot(pair_select, antenna_coords, precision=lax.Precision.HIGHEST)
    baseline_east = baseline_both[:, 0]
    baseline_north = baseline_both[:, 1]
    chan_index = (lax.axis_index("freq") * chan_count + jnp.arange(chan_count)).astype(jnp.float32)
    frequency = NU_START + NU_STEP * chan_index
    wavenum = TWO_PI * frequency / C_LIGHT
    beam_width = BEAM_SIGMA * NU_START / frequency
    own_first = lax.axis_index("lst") * time_count
    time_span = visible.shape[0] * BLOCK_T
    samples = (own_first + jnp.arange(time_span)).astype(jnp.float32)
    centre = CENTRE_START + OMEGA_STEP * samples
    seen_rows = visible.astype(jnp.float32)
    block_range = jnp.arange(seen_rows.shape[1])

    def add_block(total, east_low, north_low, bright_low, gains, offset):
        east_pos = east_low.astype(jnp.float32)
        north_pos = north_low.astype(jnp.float32)
        bright = bright_low.astype(jnp.float32)
        src_count = east_pos.shape[0]
        block_ids = (offset + jnp.arange(src_count)) // SRC_BLOCK
        onehot = (block_ids[:, None] == block_range[None, :]).astype(jnp.float32)
        seen_mask = jnp.dot(onehot, seen_rows.T, precision=lax.Precision.HIGHEST)
        seen_mask = jnp.repeat(seen_mask, BLOCK_T, axis=1) * gains.astype(jnp.float32)
        geometry = (
            baseline_east[:, None] * east_pos[None, :]
            + baseline_north[:, None] * north_pos[None, :]
        )
        phases = wavenum[:, None, None] * geometry[None]
        planes = jnp.concatenate([jnp.cos(phases), -jnp.sin(phases)], axis=1).astype(jnp.bfloat16)
        beam_gain = jnp.exp(
            -(
                (east_pos[None, :, None] - centre[None, None, :]) ** 2
                + (north_pos**2)[None, :, None]
            )
            / (2.0 * beam_width * beam_width)[:, None, None]
        )
        amplitude = ((bright * scale_norm)[None, :, None] * beam_gain * seen_mask[None]).astype(
            jnp.bfloat16
        )
        return total + jnp.einsum(
            "crs,cst->crt", planes, amplitude, preferred_element_type=jnp.float32
        )

    initial = jnp.zeros((chan_count, 2 * line_count, time_span), jnp.float32)
    east_all = lax.all_gather(sky_east, "freq", axis=0, tiled=True)
    north_all = lax.all_gather(sky_north, "freq", axis=0, tiled=True)
    bright_all = lax.all_gather(sky_flux, "freq", axis=0, tiled=True)
    gains_all = lax.all_gather(sky_scint, "freq", axis=0, tiled=True)
    whole_count = east_all.shape[0]
    group_len = math.gcd(whole_count, 512)
    group_count = whole_count // group_len

    def one_group(carry, inputs):
        east_pos, north_pos, bright, gains, group_no = inputs
        return (add_block(carry, east_pos, north_pos, bright, gains, group_no * group_len), None)

    grouped = (
        east_all.reshape(group_count, group_len),
        north_all.reshape(group_count, group_len),
        bright_all.reshape(group_count, group_len),
        gains_all.reshape(group_count, group_len, gains_all.shape[1]),
        jnp.arange(group_count),
    )
    summed_output, unused = lax.scan(one_group, initial, grouped)
    real_component = summed_output[:, :line_count]
    imaginary_component = summed_output[:, line_count:]
    fringe = (wavenum[:, None] * baseline_east[None, :])[:, :, None] * (OMEGA_STEP * samples)[
        None, None, :
    ]
    vis_real = jnp.cos(fringe) * real_component + jnp.sin(fringe) * imaginary_component
    vis_imag = jnp.cos(fringe) * imaginary_component - jnp.sin(fringe) * real_component
    visibility = jnp.stack([vis_real, vis_imag], axis=1).astype(jnp.bfloat16)
    tail_part = shifted(visibility, "lst", 1)
    toeplitz = banded_taps(filter_taps, time_count)
    own_rows = visibility.reshape(chan_count, 2 * line_count, time_count)
    tail_rows = tail_part.reshape(chan_count, 2 * line_count, TAIL)
    joined = jnp.concatenate([tail_rows, own_rows], axis=2)
    filtered = jnp.einsum("crj,cjt->crt", joined, toeplitz, preferred_element_type=jnp.float32)
    filtered = filtered.reshape(chan_count, 2, line_count, time_count).astype(jnp.bfloat16)
    return (visibility, filtered)


def solution(mesh):
    return jax.shard_map(
        shards,
        mesh=mesh,
        in_specs=(
            P(("trial", "freq")),
            P(("trial", "freq")),
            P(("trial", "freq")),
            P(("trial", "freq"), "lst"),
            P(("trial", "lst"), None),
            P(),
            P(),
            P("freq", None),
        ),
        out_specs=(
            P(("trial", "freq"), None, None, "lst"),
            P(("trial", "freq"), None, None, "lst"),
        ),
        check_vma=False,
    )
```

profile of v0, /device:TPU:0, one launch (start us, length us, event | category | flops | bytes accessed | tf_op | source)
XLA Modules:
  0.0 145.6 jit_solution(11078769584235695790)
XLA Ops:
  8.7 6.3 %all_gather.12 = bf16[4096]{0:T(1024)(128)(2,1)S(1)} all-gather(bf16[1024]{0:T(1024)(128)(2,1)} %param.10), channel_id=1, replica_groups=mesh['trial'=2,'freq'=4,'lst'=4] {'freq'}, dimensions={0}, use_global_device_ids=true | all-gather | bytes 10240 | tf_op jit(solution)/shard_map/all_gather | solution.py:105
  15.0 5.6 %all_gather.13 = bf16[4096]{0:T(1024)(128)(2,1)S(1)} all-gather(bf16[1024]{0:T(1024)(128)(2,1)} %param.11), channel_id=1, replica_groups=mesh['trial'=2,'freq'=4,'lst'=4] {'freq'}, dimensions={0}, use_global_device_ids=true | all-gather | bytes 10240 | tf_op jit(solution)/shard_map/all_gather | solution.py:106
  20.6 5.5 %all_gather.14 = bf16[4096]{0:T(1024)(128)(2,1)S(1)} all-gather(bf16[1024]{0:T(1024)(128)(2,1)} %param.12), channel_id=1, replica_groups=mesh['trial'=2,'freq'=4,'lst'=4] {'freq'}, dimensions={0}, use_global_device_ids=true | all-gather | bytes 10240 | tf_op jit(solution)/shard_map/all_gather | solution.py:107
  27.6 7.3 %all-gather.2.cloned.1.call-done = bf16[4096,256]{1,0:T(8,128)(2,1)} async-done(((bf16[1024,256]{1,0:T(8,128)(2,1)}), bf16[4096,256]{1,0:T(8,128)(2,1)}) %all-gather.2.cloned.1.call-update) | async-done | bytes 2097168 | tf_op jit(solution)/shard_map/all_gather | solution.py:108
  34.9 81.4 %while.15 = (s32[]{:T(128)}, f32[2,512,256]{2,1,0:T(8,128)}, f32[256,1]{0,1:T(1,128)S(1)}, bf16[8,512]{1,0:T(8,128)(2,1)S(1)}, f32[256,1]{0,1:T(1,128)S(1)}, /*i...) while((s32[]{:T(128)}, f32[2,512,256]{2,1,0:T(8,128)}, ...), condition=%wide.region_1.2_spmd.clone.clone.clone, body=%wide.region_0.1_spmd.clone.clone.clone.sunk | while | flops 280653344 | bytes 9864423 | solution.py:124
  35.1 4.1 %fusion.64 = (bf16[2,256,512]{2,1,0:T(8,128)(2,1)S(1)}, bf16[2,256,512]{2,1,0:T(8,128)(2,1)S(1)}) fusion(f32[256,512]{1,0:T(8,128)S(1)} %multiply_add_fusion.5, f32[2]{0:T(128)S(1)} %get-tuple-element.433), kind=kLoop, calls=%fused_computation.11.clone.1 | loop fusion | flops 1048576 | bytes 1572872 | tf_op jit(solution)/shard_map/convert.3
  41.0 1.0 constant_dynamic-slice_fusion.2
  42.4 1.6 %convolution_add_fusion.2 = f32[2,512,256]{2,1,0:T(8,128)} fusion(bf16[2,256,512]{2,1,0:T(8,128)(2,1)S(1)} %get-tuple-element.434, bf16[2,256,512]{2,1,0:T(8,128)(2,1)S(1)} %get-tuple-element.435, f32[2,512,256]{2,1,0:T(8,128)} %get-tuple-element.455, f32[512,256]{1,0:T(8,128)S(1)} %copy.25, f32[2]{0:T(128)S(1)} %get-tuple-element.436, ...), kind=kOutput, calls=%fused_computation.6.clone.1 | convolution fusion | flops 272105472 | bytes 4196361 | tf_op jit(solution)/shard_map/while/body/eval_jaxpr/crs,cst->crt/dot_general | solution.py:100
  44.2 4.1 %fusion.64 = (bf16[2,256,512]{2,1,0:T(8,128)(2,1)S(1)}, bf16[2,256,512]{2,1,0:T(8,128)(2,1)S(1)}) fusion(f32[256,512]{1,0:T(8,128)S(1)} %multiply_add_fusion.5, f32[2]{0:T(128)S(1)} %get-tuple-element.433), kind=kLoop, calls=%fused_computation.11.clone.1 | loop fusion | flops 1048576 | bytes 1572872 | tf_op jit(solution)/shard_map/convert.3
  50.1 1.0 constant_dynamic-slice_fusion.2
  51.5 2.8 %convolution_add_fusion.2 = f32[2,512,256]{2,1,0:T(8,128)} fusion(bf16[2,256,512]{2,1,0:T(8,128)(2,1)S(1)} %get-tuple-element.434, bf16[2,256,512]{2,1,0:T(8,128)(2,1)S(1)} %get-tuple-element.435, f32[2,512,256]{2,1,0:T(8,128)} %get-tuple-element.455, f32[512,256]{1,0:T(8,128)S(1)} %copy.25, f32[2]{0:T(128)S(1)} %get-tuple-element.436, ...), kind=kOutput, calls=%fused_computation.6.clone.1 | convolution fusion | flops 272105472 | bytes 4196361 | tf_op jit(solution)/shard_map/while/body/eval_jaxpr/crs,cst->crt/dot_general | solution.py:100
  54.6 4.1 %fusion.64 = (bf16[2,256,512]{2,1,0:T(8,128)(2,1)S(1)}, bf16[2,256,512]{2,1,0:T(8,128)(2,1)S(1)}) fusion(f32[256,512]{1,0:T(8,128)S(1)} %multiply_add_fusion.5, f32[2]{0:T(128)S(1)} %get-tuple-element.433), kind=kLoop, calls=%fused_computation.11.clone.1 | loop fusion | flops 1048576 | bytes 1572872 | tf_op jit(solution)/shard_map/convert.3
  61.9 2.8 %convolution_add_fusion.2 = f32[2,512,256]{2,1,0:T(8,128)} fusion(bf16[2,256,512]{2,1,0:T(8,128)(2,1)S(1)} %get-tuple-element.434, bf16[2,256,512]{2,1,0:T(8,128)(2,1)S(1)} %get-tuple-element.435, f32[2,512,256]{2,1,0:T(8,128)} %get-tuple-element.455, f32[512,256]{1,0:T(8,128)S(1)} %copy.25, f32[2]{0:T(128)S(1)} %get-tuple-element.436, ...), kind=kOutput, calls=%fused_computation.6.clone.1 | convolution fusion | flops 272105472 | bytes 4196361 | tf_op jit(solution)/shard_map/while/body/eval_jaxpr/crs,cst->crt/dot_general | solution.py:100
  64.9 4.1 %fusion.64 = (bf16[2,256,512]{2,1,0:T(8,128)(2,1)S(1)}, bf16[2,256,512]{2,1,0:T(8,128)(2,1)S(1)}) fusion(f32[256,512]{1,0:T(8,128)S(1)} %multiply_add_fusion.5, f32[2]{0:T(128)S(1)} %get-tuple-element.433), kind=kLoop, calls=%fused_computation.11.clone.1 | loop fusion | flops 1048576 | bytes 1572872 | tf_op jit(solution)/shard_map/convert.3
  70.8 1.0 constant_dynamic-slice_fusion.2
  72.2 2.8 %convolution_add_fusion.2 = f32[2,512,256]{2,1,0:T(8,128)} fusion(bf16[2,256,512]{2,1,0:T(8,128)(2,1)S(1)} %get-tuple-element.434, bf16[2,256,512]{2,1,0:T(8,128)(2,1)S(1)} %get-tuple-element.435, f32[2,512,256]{2,1,0:T(8,128)} %get-tuple-element.455, f32[512,256]{1,0:T(8,128)S(1)} %copy.25, f32[2]{0:T(128)S(1)} %get-tuple-element.436, ...), kind=kOutput, calls=%fused_computation.6.clone.1 | convolution fusion | flops 272105472 | bytes 4196361 | tf_op jit(solution)/shard_map/while/body/eval_jaxpr/crs,cst->crt/dot_general | solution.py:100
  75.2 4.1 %fusion.64 = (bf16[2,256,512]{2,1,0:T(8,128)(2,1)S(1)}, bf16[2,256,512]{2,1,0:T(8,128)(2,1)S(1)}) fusion(f32[256,512]{1,0:T(8,128)S(1)} %multiply_add_fusion.5, f32[2]{0:T(128)S(1)} %get-tuple-element.433), kind=kLoop, calls=%fused_computation.11.clone.1 | loop fusion | flops 1048576 | bytes 1572872 | tf_op jit(solution)/shard_map/convert.3
  82.5 2.8 %convolution_add_fusion.2 = f32[2,512,256]{2,1,0:T(8,128)} fusion(bf16[2,256,512]{2,1,0:T(8,128)(2,1)S(1)} %get-tuple-element.434, bf16[2,256,512]{2,1,0:T(8,128)(2,1)S(1)} %get-tuple-element.435, f32[2,512,256]{2,1,0:T(8,128)} %get-tuple-element.455, f32[512,256]{1,0:T(8,128)S(1)} %copy.25, f32[2]{0:T(128)S(1)} %get-tuple-element.436, ...), kind=kOutput, calls=%fused_computation.6.clone.1 | convolution fusion | flops 272105472 | bytes 4196361 | tf_op jit(solution)/shard_map/while/body/eval_jaxpr/crs,cst->crt/dot_general | solution.py:100
  85.6 4.1 %fusion.64 = (bf16[2,256,512]{2,1,0:T(8,128)(2,1)S(1)}, bf16[2,256,512]{2,1,0:T(8,128)(2,1)S(1)}) fusion(f32[256,512]{1,0:T(8,128)S(1)} %multiply_add_fusion.5, f32[2]{0:T(128)S(1)} %get-tuple-element.433), kind=kLoop, calls=%fused_computation.11.clone.1 | loop fusion | flops 1048576 | bytes 1572872 | tf_op jit(solution)/shard_map/convert.3
  92.9 2.8 %convolution_add_fusion.2 = f32[2,512,256]{2,1,0:T(8,128)} fusion(bf16[2,256,512]{2,1,0:T(8,128)(2,1)S(1)} %get-tuple-element.434, bf16[2,256,512]{2,1,0:T(8,128)(2,1)S(1)} %get-tuple-element.435, f32[2,512,256]{2,1,0:T(8,128)} %get-tuple-element.455, f32[512,256]{1,0:T(8,128)S(1)} %copy.25, f32[2]{0:T(128)S(1)} %get-tuple-element.436, ...), kind=kOutput, calls=%fused_computation.6.clone.1 | convolution fusion | flops 272105472 | bytes 4196361 | tf_op jit(solution)/shard_map/while/body/eval_jaxpr/crs,cst->crt/dot_general | solution.py:100
  95.9 4.1 %fusion.64 = (bf16[2,256,512]{2,1,0:T(8,128)(2,1)S(1)}, bf16[2,256,512]{2,1,0:T(8,128)(2,1)S(1)}) fusion(f32[256,512]{1,0:T(8,128)S(1)} %multiply_add_fusion.5, f32[2]{0:T(128)S(1)} %get-tuple-element.433), kind=kLoop, calls=%fused_computation.11.clone.1 | loop fusion | flops 1048576 | bytes 1572872 | tf_op jit(solution)/shard_map/convert.3
  103.2 2.8 %convolution_add_fusion.2 = f32[2,512,256]{2,1,0:T(8,128)} fusion(bf16[2,256,512]{2,1,0:T(8,128)(2,1)S(1)} %get-tuple-element.434, bf16[2,256,512]{2,1,0:T(8,128)(2,1)S(1)} %get-tuple-element.435, f32[2,512,256]{2,1,0:T(8,128)} %get-tuple-element.455, f32[512,256]{1,0:T(8,128)S(1)} %copy.25, f32[2]{0:T(128)S(1)} %get-tuple-element.436, ...), kind=kOutput, calls=%fused_computation.6.clone.1 | convolution fusion | flops 272105472 | bytes 4196361 | tf_op jit(solution)/shard_map/while/body/eval_jaxpr/crs,cst->crt/dot_general | solution.py:100
  106.2 4.1 %fusion.64 = (bf16[2,256,512]{2,1,0:T(8,128)(2,1)S(1)}, bf16[2,256,512]{2,1,0:T(8,128)(2,1)S(1)}) fusion(f32[256,512]{1,0:T(8,128)S(1)} %multiply_add_fusion.5, f32[2]{0:T(128)S(1)} %get-tuple-element.433), kind=kLoop, calls=%fused_computation.11.clone.1 | loop fusion | flops 1048576 | bytes 1572872 | tf_op jit(solution)/shard_map/convert.3
  113.5 2.8 %convolution_add_fusion.2 = f32[2,512,256]{2,1,0:T(8,128)} fusion(bf16[2,256,512]{2,1,0:T(8,128)(2,1)S(1)} %get-tuple-element.434, bf16[2,256,512]{2,1,0:T(8,128)(2,1)S(1)} %get-tuple-element.435, f32[2,512,256]{2,1,0:T(8,128)} %get-tuple-element.455, f32[512,256]{1,0:T(8,128)S(1)} %copy.25, f32[2]{0:T(128)S(1)} %get-tuple-element.436, ...), kind=kOutput, calls=%fused_computation.6.clone.1 | convolution fusion | flops 272105472 | bytes 4196361 | tf_op jit(solution)/shard_map/while/body/eval_jaxpr/crs,cst->crt/dot_general | solution.py:100
  116.4 3.7 %fusion.37 = (bf16[2,1,256,256]{3,2,1,0:T(8,128)(2,1)S(1)}, bf16[2,1,256,256]{3,2,1,0:T(8,128)(2,1)S(1)}) fusion(f32[2,512,256]{2,1,0:T(8,128)} %get-tuple-element.176, f32[256]{0:T(256)S(1)} %convert_multiply_fusion.1, f32[2,256]{1,0:T(2,128)S(1)} %broadcast_multiply_fusion.1), kind=kLoop, calls=%fused_computation.59 | loop fusion | flops 1179648 | bytes 1575936 | tf_op jit(solution)/shard_map/stack | solution.py:132
  120.9 4.2 %collective-permute-start = (bf16[2,2,256,256]{3,2,1,0:T(8,128)(2,1)}, bf16[2,2,256,256]{3,2,1,0:T(8,128)(2,1)}, u32[]{:S(2)}, u32[]{:S(2)}) collective-permute-start(bf16[2,2,256,256]{3,2,1,0:T(8,128)(2,1)} %maximum_convert_fusion), channel_id=1, source_target_pairs={{0,1},{1,2},{2,3},{4,5},{5,6},{6,7},{8,9},{9,10},{10,11},{12,13},{... | collective-permute-start | bytes 1572872 | tf_op jit(solution)/shard_map/ppermute | solution.py:25
  125.4 1.6 %copy.21 = bf16[1,2,512,768]{3,1,2,0:T(2,128)(2,1)S(1)} copy(bf16[1,2,512,768]{3,2,1,0:T(8,128)(2,1)S(1)} %broadcast_bitcast_fusion) | data formatting | bytes 3145728
  127.0 1.1 slice.34
  128.2 1.0 reshape.289
  129.2 3.8 %reshape.277 = bf16[2,512,767]{2,1,0:T(8,128)(2,1)S(1)} reshape(bf16[785408]{0:T(1024)(128)(2,1)S(1)} %reshape.289) | data formatting | bytes 3141632 | tf_op jit(solution)/shard_map/reshape | solution.py:38
  133.0 3.2 %collective-permute-done = bf16[2,2,256,256]{3,2,1,0:T(8,128)(2,1)} collective-permute-done((bf16[2,2,256,256]{3,2,1,0:T(8,128)(2,1)}, bf16[2,2,256,256]{3,2,1,0:T(8,128)(2,1)}, u32[]{:S(2)}, u32[]{:S(2)}) %collective-permute-start) | collective-permute-done | bytes 524320 | tf_op jit(solution)/shard_map/ppermute | solution.py:25
  136.2 2.5 %convolution_convert_fusion = bf16[2,512,256]{2,1,0:T(8,128)(2,1)} fusion(bf16[2,512,256]{2,1,0:T(8,128)(2,1)} %bitcast.8, bf16[2,512,256]{2,1,0:T(8,128)(2,1)} %bitcast.7, bf16[2,512,767]{2,1,0:T(8,128)(2,1)S(1)} %reshape.277), kind=kOutput, calls=%fused_computation.46 | convolution fusion | flops 270794752 | bytes 2097152 | tf_op jit(solution)/shard_map/crj,cjt->crt/dot_general | solution.py:138
  (126 shorter events, 22.8 us)
Async XLA Ops:
  7.2 19.8 %copy-start = (f32[350,2]{0,1:T(2,128)S(1)}, f32[350,2]{0,1:T(2,128)}, u32[]{:S(2)}) copy-start(f32[350,2]{0,1:T(2,128)} %param.15) | copy-start | bytes 8404
  7.2 27.7 %all-gather.2.cloned.1.call-start = ((), (), s32[]{:S(2)}) async-start(), calls=%async_computation | async-start | bytes 2621440 | tf_op jit(solution)/shard_map/all_gather | solution.py:108
  116.4 8.8 %copy-start.1 = (bf16[2,257]{1,0:T(2,128)(2,1)S(1)}, bf16[2,257]{1,0:T(2,128)(2,1)}, u32[]{:S(2)}) copy-start(bf16[2,257]{1,0:T(2,128)(2,1)} %param.17) | copy-start | bytes 3088
  120.9 15.3 %collective-permute-start = (bf16[2,2,256,256]{3,2,1,0:T(8,128)(2,1)}, bf16[2,2,256,256]{3,2,1,0:T(8,128)(2,1)}, u32[]{:S(2)}, u32[]{:S(2)}) collective-permute-start(bf16[2,2,256,256]{3,2,1,0:T(8,128)(2,1)} %maximum_convert_fusion), channel_id=1, source_target_pairs={{0,1},{1,2},{2,3},{4,5},{5,6},{6,7},{8,9},{9,10},{10,11},{12,13},{... | collective-permute-start | bytes 1572872 | tf_op jit(solution)/shard_map/ppermute | solution.py:25
Sparse Core Ops, SparseCore 0:
  9.5 25.3 all-gather.1
where the time goes:
time: 147 us; the launch traced here: 146 us
  other arithmetic  41.7 us (28%)
  matrix products  27.3 us (19%)
  local copies, waits for them, and re-layouts  23.9 us (16%)
  blocking collectives  17.4 us (12%)
  between operations  14.1 us (10%)
  waiting for transfers between devices  11.2 us (8%)
  loops' own time  5.71 us (4%)
  starting transfers between devices  4.23 us (3%)
    another operation x8, other arithmetic  32.6 us
    dot_general x8, matrix products, add_block(): jnp.einsum('crs,cst->crt', planes, amplitude, preferred_element_type=jnp....  21.5 us
    dynamic_slice x24, local copies, waits for them, and re-layouts, shards(): summed_output, unused = lax.scan(one_group, initial, grouped)  13.8 us
    all_gather x1, waiting for transfers between devices, shards(): gains_all = lax.all_gather(sky_scint, 'freq', axis=0, tiled=True)  7.3 us
    all_gather x1, blocking collectives, shards(): east_all = lax.all_gather(sky_east, 'freq', axis=0, tiled=True)  6.35 us
    another operation x1, loops' own time, shards(): summed_output, unused = lax.scan(one_group, initial, grouped)  5.71 us
    all_gather x1, blocking collectives, shards(): north_all = lax.all_gather(sky_north, 'freq', axis=0, tiled=True)  5.58 us
    all_gather x1, blocking collectives, shards(): bright_all = lax.all_gather(sky_flux, 'freq', axis=0, tiled=True)  5.5 us
  transfers between devices with their start and end apart: 2, of which 2 were waited for; matrix products, arithmetic and copies ran while one was open for 7% of the time, Pallas kernels for 0%

commit v1 on v0

v1 whole, which is shorter than its diff:
```python
import functools
import math

import jax
import jax.numpy as jnp
import numpy as np
from jax import lax
from jax.experimental import pallas as pl
from jax.experimental.pallas import tpu as pltpu
from jax.sharding import PartitionSpec as P

SRC_BLOCK = 128
TAIL = 256
BLOCK_T = 8

C_LIGHT = 299792458.0
NU_START = 150000000.0
NU_STEP = 97656.25
OMEGA_STEP = 4.37526e-05
BEAM_SIGMA = 0.35
CENTRE_START = -0.045
LOG2E = math.log2(math.e)
ROUNDER = 1.5 * 2.0**23
HIDDEN = -1024.0
ROWS = 16
GROUPS = 4
CHUNKS = 4
TILE = 256
MESH = pl.DeviceIdType.MESH
F32 = jnp.float32
BF16 = jnp.bfloat16


def fit_even(fun, reach, degree):
    nodes = np.cos((np.arange(400) + 0.5) * np.pi / 400)
    z = 0.5 * reach * reach * (nodes + 1.0)
    cheb = np.polynomial.chebyshev.Chebyshev.fit(z, fun(np.sqrt(z)), degree, domain=[0.0, reach * reach])
    return [float(c) for c in cheb.convert(kind=np.polynomial.Polynomial).coef]


def cos_turn(x):
    return np.cos(2.0 * np.pi * x)


def sin_turn(x):
    return np.sin(2.0 * np.pi * x) / x


COS_FULL = fit_even(cos_turn, 0.5, 5)
SIN_FULL = fit_even(sin_turn, 0.5, 5)
STEP_REACH = 0.12
COS_STEP = fit_even(cos_turn, STEP_REACH, 3)
SIN_STEP = fit_even(sin_turn, STEP_REACH, 2)


def horner(coefs, z):
    total = coefs[-1] * z + coefs[-2]
    for c in coefs[-3::-1]:
        total = total * z + c
    return total


def sincos_turns(turns):
    r = turns - ((turns + ROUNDER) - ROUNDER)
    z = r * r
    return horner(COS_FULL, z), horner(SIN_FULL, z) * r


def sincos_step(r):
    z = r * r
    return horner(COS_STEP, z), horner(SIN_STEP, z) * r


def pieces(x):
    high = x.astype(BF16).astype(F32)
    middle = (x - high).astype(BF16).astype(F32)
    low = (x - high - middle).astype(BF16).astype(F32)
    return high, middle, low


def rowdot(a, b):
    return lax.dot_general(a, b, (((0,), (0,)), ((), ())), preferred_element_type=F32)


def kernel(
    dims,
    sky_ref, scint_ref, visible_ref, coords_ref, pairs_ref, taps_ref,
    vis_ref, out_ref,
    sky_all, gains_all, phase_rows, beam_rows, planes, amps, mask_rows, coefs, lines, toep, tap_rows, tail,
    sky_send, sky_recv, near_send, near_recv, far_send, far_recv, fwd_send, fwd_recv, halo_send, halo_recv,
):
    n_freq, n_lst, chans, total_sources = dims
    local_src = scint_ref.shape[0]
    times = scint_ref.shape[1]
    count = pairs_ref.shape[0]
    group = count // GROUPS
    chips = n_freq // 2
    part = local_src // CHUNKS
    me = lax.axis_index("freq")
    lst = lax.axis_index("lst")
    chip, core = me // 2, me % 2
    partner = chip * 2 + (1 - core)

    barrier = pltpu.get_barrier_semaphore()
    for d in range(1, n_freq):
        pl.semaphore_signal(barrier, inc=1, device_id={"freq": (me + d) % n_freq}, device_id_type=MESH)

    for d in (1, n_lst - 1):
        pl.semaphore_signal(barrier, inc=1, device_id={"lst": (lst + d) % n_lst}, device_id_type=MESH)
    pl.semaphore_wait(barrier, n_freq + 1)

    def send(src, dst, ssem, rsem, to):
        return pltpu.make_async_remote_copy(
            src_ref=src, dst_ref=dst, send_sem=ssem, recv_sem=rsem, device_id=to, device_id_type=MESH
        )

    sky_copies = [
        send(sky_ref, sky_all.at[me], sky_send.at[d - 1], sky_recv.at[d - 1], {"freq": (me + d) % n_freq})
        for d in range(1, n_freq)
    ]
    for copy in sky_copies:
        copy.start()
    far_copies = []
    for k in range(CHUNKS):
        rows = pl.ds(k * part, part)
        for d in range(1, chips):
            to = ((chip + d) % chips) * 2 + core
            copy = send(
                scint_ref.at[rows], gains_all.at[me, rows], far_send.at[d - 1, k], far_recv.at[d - 1, k], {"freq": to}
            )
            copy.start()
            far_copies.append(copy)
    near_copy = send(scint_ref, gains_all.at[me], near_send.at[0], near_recv.at[0], {"freq": partner})
    near_copy.start()
    sky_all[me] = sky_ref[...]

    first_chan = (me * chans).astype(F32)
    nus = [NU_START + NU_STEP * (first_chan + c) for c in range(chans)]

    antennas = coords_ref.shape[0]
    ids = lax.broadcasted_iota(jnp.int32, (count, antennas), 1)
    select = (pairs_ref[:, 0:1] == ids).astype(F32) - (pairs_ref[:, 1:2] == ids).astype(F32)
    both = jnp.dot(select, coords_ref[...], precision=lax.Precision.HIGHEST, preferred_element_type=F32)
    east, north = both[:, 0:1], both[:, 1:2]
    lane = lax.broadcasted_iota(jnp.int32, (count, ROWS), 1)
    pair_value = jnp.where(lane < 3, east, jnp.where(lane < 6, north, 0.0))

    def coef_rows(scale):
        high, middle, low = pieces(pair_value * scale)
        picked = jnp.where((lane == 0) | (lane == 3), high, jnp.where((lane == 1) | (lane == 4), middle, low))
        return picked.astype(BF16)

    main = coef_rows(nus[0] * (1.0 / C_LIGHT))
    step = coef_rows(NU_STEP / C_LIGHT)
    for g in range(GROUPS):
        coefs[g, 0:group, :] = main[g * group : (g + 1) * group]
        coefs[g, group : 2 * group, :] = step[g * group : (g + 1) * group]
    lines[...] = jnp.broadcast_to(east, lines.shape)

    t_blocks = visible_ref.shape[0]
    spread = (
        lax.broadcasted_iota(jnp.int32, (t_blocks, times), 1) // BLOCK_T
        == lax.broadcasted_iota(jnp.int32, (t_blocks, times), 0)
    ).astype(BF16)
    hidden = ((1.0 - visible_ref[...].astype(F32)) * HIDDEN).astype(BF16)
    mask_rows[...] = rowdot(hidden, spread)

    tap_rows[...] = jnp.zeros_like(tap_rows)
    tap_rows[0:chans, 0 : TAIL + 1] = taps_ref[...].astype(F32)
    for c in range(chans):
        wide = jnp.broadcast_to(tap_rows[c : c + 1, :], (TAIL + times, TAIL + times))
        skewed = pltpu.roll(wide, 0, 1, stride=1, stride_axis=0)
        toep[c] = skewed[:, TAIL:].astype(BF16)

    samples = (lst * times + lax.broadcasted_iota(jnp.int32, (1, times), 1)).astype(F32)
    centre = CENTRE_START + OMEGA_STEP * samples
    row_id = lax.broadcasted_iota(jnp.int32, (ROWS, times), 0)
    beam_right = []
    for c in range(chans):
        ratio = nus[c] * (1.0 / (BEAM_SIGMA * NU_START))
        half = 0.5 * LOG2E * ratio * ratio
        ch, cm, cl = pieces(centre * (2.0 * half))
        gh, gm, gl = pieces(centre * centre * (-half))
        table = jnp.where((row_id >= 3) & (row_id < 6), 1.0, 0.0)
        for at, row in ((0, ch), (1, cm), (2, cl), (6, gh), (7, gm), (8, gl)):
            table = jnp.where(row_id == at, row, table)
        beam_right.append(table)

    for copy in sky_copies:
        copy.wait()

    src_row = lax.broadcasted_iota(jnp.int32, (ROWS, local_src), 0)

    @pl.loop(0, n_freq)
    def _(j):
        l, m, flux = sky_all[j, 0:1, :], sky_all[j, 1:2, :], sky_all[j, 2:3, :]
        cols = pl.ds(pl.multiple_of(j * local_src, local_src), local_src)
        phase_rows[:, cols] = jnp.where(src_row < 3, l, jnp.where(src_row < 6, m, 0.0)).astype(BF16)
        log_flux = jnp.log(flux * (1.0 / math.sqrt(total_sources))) * LOG2E
        for c in range(chans):
            ratio = nus[c] * (1.0 / (BEAM_SIGMA * NU_START))
            half = 0.5 * LOG2E * ratio * ratio
            bh, bm, bl = pieces(log_flux - (l * l + m * m) * half)
            table = jnp.where(src_row < 3, l, 1.0)
            for at, row in ((3, bh), (4, bm), (5, bl)):
                table = jnp.where(src_row == at, row, table)
            beam_rows[c, :, cols] = jnp.where(src_row < 10, table, 0.0).astype(BF16)

    def trig(g):
        @pl.loop(0, total_sources // TILE)
        def _(i):
            cols = pl.ds(pl.multiple_of(i * TILE, TILE), TILE)
            turns = jnp.dot(coefs[g], phase_rows[:, cols], preferred_element_type=F32)
            co, si = sincos_turns(turns[:group])
            cd, sd = sincos_step(turns[group:])
            for c in range(chans):
                if c > 0:
                    co, si = co * cd - si * sd, si * cd + co * sd
                planes[g % 2, c, 0:group, cols] = co.astype(BF16)
                planes[g % 2, c, group : 2 * group, cols] = (-si).astype(BF16)

    def amplitudes(block, gains):
        @pl.loop(0, local_src // SRC_BLOCK)
        def _(k):
            at = pl.multiple_of(block * local_src + k * SRC_BLOCK, SRC_BLOCK)
            mask = mask_rows[pl.ds(block * (local_src // SRC_BLOCK) + k, 1), :]
            gain = gains(pl.ds(pl.multiple_of(k * SRC_BLOCK, SRC_BLOCK), SRC_BLOCK)).astype(F32)
            for c in range(chans):
                right = jnp.where(row_id == 9, mask, beam_right[c]).astype(BF16)
                power = rowdot(beam_rows[c, :, pl.ds(at, SRC_BLOCK)], right)
                amps[c, pl.ds(at, SRC_BLOCK), :] = (jnp.exp2(power) * gain).astype(BF16)

    def multiply(g):
        rows = pl.ds(pl.multiple_of(g * group, group), group)
        for c in range(chans):
            summed = jnp.dot(planes[g % 2, c], amps[c], preferred_element_type=F32)
            real, imag = summed[:group], summed[group:]
            scale = nus[c] * (OMEGA_STEP / C_LIGHT)
            co, si = sincos_turns((lines[rows, :] * scale) * samples)
            vis_ref[c, 0, rows, :] = (co * real + si * imag).astype(BF16)
            vis_ref[c, 1, rows, :] = (co * imag - si * real).astype(BF16)

    def halo(g):
        rows = pl.ds(pl.multiple_of(g * group, group), group)
        return send(
            vis_ref.at[:, :, rows, :], tail.at[:, :, rows, :], halo_send.at[g], halo_recv.at[g], {"lst": (lst + 1) % n_lst}
        )

    def send_group(g):
        @pl.when(lst < n_lst - 1)
        def _():
            halo(g).start()

    def far(d, k):
        rows = pl.ds(k * part, part)
        src = ((chip + chips - d) % chips) * 2 + core
        return send(
            gains_all.at[src, rows], gains_all.at[src, rows], fwd_send.at[d - 1, k], fwd_recv.at[d - 1, k], {"freq": partner}
        )

    def forward(k):
        for d in range(1, chips):
            far_copies[k * (chips - 1) + d - 1].wait_recv()
            far(d, k).start()

    trig(0)
    forward(0)
    amplitudes(me, lambda rows: scint_ref[rows, :])
    near_copy.wait()
    forward(1)
    amplitudes(partner, lambda rows: gains_all[partner, rows, :])
    trig(1)
    for k in range(2, CHUNKS):
        forward(k)
    for d in range(1, chips):
        src = ((chip + chips - d) % chips) * 2 + core
        amplitudes(src, lambda rows, src=src: gains_all[src, rows, :])
    for k in range(CHUNKS):
        for d in range(1, chips):
            far(d, k).wait()
    for d in range(1, chips):
        src = ((chip + chips - d) % chips) * 2 + (1 - core)
        amplitudes(src, lambda rows, src=src: gains_all[src, rows, :])
    for copy in far_copies:
        copy.wait_send()

    @pl.loop(0, GROUPS)
    def _(g):
        multiply(g)
        send_group(g)

        @pl.when(g + 2 < GROUPS)
        def _():
            trig(g + 2)

    @pl.when(lst == 0)
    def _():
        tail[...] = jnp.zeros_like(tail)

    for g in range(GROUPS):
        @pl.when(lst > 0)
        def _():
            halo(g).wait_recv()

        rows = slice(g * group, (g + 1) * group)
        for c in range(chans):
            for r in range(2):
                total = jnp.dot(tail[c, r, rows, :], toep[c, :TAIL, :], preferred_element_type=F32)
                total = total + jnp.dot(vis_ref[c, r, rows, :], toep[c, TAIL:, :], preferred_element_type=F32)
                out_ref[c, r, rows, :] = total.astype(BF16)

    @pl.when(lst < n_lst - 1)
    def _():
        for g in range(GROUPS):
            halo(g).wait_send()


def shards(n_freq, n_lst, sky_east, sky_north, sky_flux, sky_scint, visible, antenna_coords, baseline_antennas, filter_taps):
    chans = filter_taps.shape[0]
    local_src, times = sky_scint.shape
    total = local_src * n_freq
    count = baseline_antennas.shape[0]
    group = count // GROUPS
    chips = n_freq // 2
    sky = jnp.stack([sky_east, sky_north, sky_flux, sky_flux]).astype(F32)
    shape = jax.ShapeDtypeStruct((chans, 2, count, times), BF16)
    vmem = pl.BlockSpec(memory_space=pltpu.VMEM)
    dma = pltpu.SemaphoreType.DMA
    far = max(chips - 1, 1)
    return pl.pallas_call(
        functools.partial(kernel, (n_freq, n_lst, chans, total)),
        out_shape=(shape, shape),
        in_specs=[vmem] * 6,
        out_specs=(vmem, vmem),
        scratch_shapes=[
            pltpu.VMEM((n_freq, 4, local_src), F32),
            pltpu.VMEM((n_freq, local_src, times), BF16),
            pltpu.VMEM((ROWS, total), BF16),
            pltpu.VMEM((chans, ROWS, total), BF16),
            pltpu.VMEM((2, chans, 2 * group, total), BF16),
            pltpu.VMEM((chans, total, times), BF16),
            pltpu.VMEM((visible.shape[1], times), F32),
            pltpu.VMEM((GROUPS, 2 * group, ROWS), BF16),
            pltpu.VMEM((count, times), F32),
            pltpu.VMEM((chans, TAIL + times, times), BF16),
            pltpu.VMEM((8, TAIL + times), F32),
            pltpu.VMEM((chans, 2, count, TAIL), BF16),
            dma((n_freq - 1,)), dma((n_freq - 1,)),
            dma((1,)), dma((1,)),
            dma((far, CHUNKS)), dma((far, CHUNKS)),
            dma((far, CHUNKS)), dma((far, CHUNKS)),
            dma((GROUPS,)), dma((GROUPS,)),
        ],
        compiler_params=pltpu.CompilerParams(
            collective_id=0, has_side_effects=True, vmem_limit_bytes=64000000
        ),
    )(sky, sky_scint, visible, antenna_coords, baseline_antennas, filter_taps)


def solution(mesh):
    return jax.shard_map(
        functools.partial(shards, mesh.shape["freq"], mesh.shape["lst"]),
        mesh=mesh,
        in_specs=(
            P(("trial", "freq")),
            P(("trial", "freq")),
            P(("trial", "freq")),
            P(("trial", "freq"), "lst"),
            P(("trial", "lst"), None),
            P(),
            P(),
            P("freq", None),
        ),
        out_specs=(
            P(("trial", "freq"), None, None, "lst"),
            P(("trial", "freq"), None, None, "lst"),
        ),
        check_vma=False,
    )
```

time: 147 us -> 49 us (0.33)
  Pallas kernels: 0 us -> 41.7 us
  other arithmetic: 41.7 us -> 0.63 us
  matrix products: 27.3 us -> 0 us
  local copies, waits for them, and re-layouts: 23.9 us -> 5.77 us
  blocking collectives: 17.4 us -> 0 us
  between operations: 14.1 us -> 0.67 us
  waiting for transfers between devices: 11.2 us -> 0 us
  loops' own time: 5.71 us -> 0 us
  starting transfers between devices: 4.23 us -> 0 us
    pallas_call x0 -> x1, Pallas kernels: none -> 41.7 us  [shards(): pl.pallas_call(functools.partial(kernel, (n_freq, n_lst, chans, total)),...]
    another operation x9 -> x0, other arithmetic: 36.3 us -> none
    dot_general x18 -> x0, matrix products: 27.3 us -> none  [the longest x8 21.5 us: add_block(): jnp.einsum('crs,cst->crt', planes, amplitude, preferred_element_type=jnp....]
    all_gather x3 -> x0, blocking collectives: 17.4 us -> none  [the longest x1 6.35 us: shards(): east_all = lax.all_gather(sky_east, 'freq', axis=0, tiled=True)]
    dynamic_slice x24 -> x0, local copies, waits for them, and re-layouts: 13.8 us -> none  [shards(): summed_output, unused = lax.scan(one_group, initial, grouped)]
    all_gather x1 -> x0, waiting for transfers between devices: 7.3 us -> none  [shards(): gains_all = lax.all_gather(sky_scint, 'freq', axis=0, tiled=True)]
    another operation x1 -> x0, loops' own time: 5.71 us -> none  [shards(): summed_output, unused = lax.scan(one_group, initial, grouped)]
    ppermute x1 -> x0, starting transfers between devices: 4.19 us -> none  [shifted(): return lax.ppermute(block, axis, route)]
  transfers between devices with their start and end apart: 2 -> 0, of which waited for: 2 -> 0; matrix products, arithmetic and copies ran while one was open for 7% -> 0% of each run, Pallas kernels for 0% -> 0%
where the time goes in v1:
time: 49 us; the launch traced here: 48.8 us
  Pallas kernels  41.7 us (85%)
  local copies, waits for them, and re-layouts  5.77 us (12%)
  between operations  0.67 us (1%)
  other arithmetic  0.63 us (1%)
    pallas_call x1, Pallas kernels, shards(): pl.pallas_call(functools.partial(kernel, (n_freq, n_lst, chans, total)),...  41.7 us
    unnamed x14, local copies, waits for them, and re-layouts  5.07 us

profile of v1, /device:TPU:0, one launch (start us, length us, event | category | flops | bytes accessed | tf_op | source)
XLA Modules:
  0.0 48.8 jit_solution(8593595962652925406)
XLA Ops:
  0.6 0.0 copy-start.3
  0.6 0.7 %stack.13 = bf16[1,1024]{1,0:T(2,128)(2,1)S(1)} reshape(bf16[1024]{0:T(1024)(128)(2,1)} %param.8) | data formatting | bytes 4096 | tf_op jit(solution)/shard_map/stack | solution.py:325
  1.3 0.0 copy-done.3
  1.3 0.0 copy-start.4
  1.4 0.7 %copy-done.4 = bf16[1024]{0:T(1024)(128)(2,1)S(1)} copy-done((bf16[1024]{0:T(1024)(128)(2,1)S(1)}, bf16[1024]{0:T(1024)(128)(2,1)}, u32[]{:S(2)}) %copy-start.4) | copy-done | bytes 2072
  2.0 0.0 copy-start.2
  2.0 0.6 %maximum_convert_fusion.sky_ref = f32[4,1024]{1,0:T(4,128)} fusion(bf16[1,1024]{1,0:T(2,128)(2,1)S(1)} %stack.15, bf16[1,1024]{1,0:T(2,128)(2,1)S(1)} %stack.14, bf16[1,1024]{1,0:T(2,128)(2,1)S(1)} %stack.13), kind=kLoop, calls=%fused_computation | loop fusion | flops 32768 | bytes 22528 | tf_op jit(solution)/shard_map/convert_element_type | solution.py:325
  2.7 0.1 copy-done.2
  2.7 0.0 copy-start.1
  2.7 0.8 %copy.11.pairs_ref = s32[256,2]{1,0:T(8,128)} copy(s32[256,2]{0,1:T(2,128)S(1)} %copy-done.2) | data formatting | bytes 4096 | tf_op args[6]
  3.5 0.0 copy-done.1
  3.5 0.8 %copy.10.coords_ref = f32[350,2]{1,0:T(8,128)} copy(f32[350,2]{0,1:T(2,128)S(1)} %copy-done.1) | data formatting | bytes 5600 | tf_op args[5]
  4.3 41.7 %shard_map.95 = (bf16[2,2,256,256]{3,2,1,0:T(8,128)(2,1)}, bf16[2,2,256,256]{3,2,1,0:T(8,128)(2,1)}) custom-call(f32[4,1024]{1,0:T(4,128)} %maximum_convert_fusion.sky_ref, bf16[1024,256]{1,0:T(8,128)(2,1)} %scint_ref.1, s32[32,32]{1,0:T(8,128)} %visible_ref.1, f32[350,2]{1,0:T(8,128)} %copy.10.coords_ref, s32[256,2]{1,0:T(8,128)} %copy.11.pairs_ref, ...), custom_call_target="tpu_custom_call" | custom-call | tf_op jit(solution)/shard_map/pallas_call | solution.py:330
  46.1 0.0 copy-start
  46.1 1.9 %copy.14 = bf16[2,2,256,256]{3,2,1,0:T(8,128)(2,1)} copy(bf16[2,2,256,256]{3,2,1,0:T(8,128)(2,1)} %get-tuple-element.4) | data formatting | bytes 1048576
  48.0 0.0 copy-done
  48.0 0.8 %copy.15 = bf16[2,2,256,256]{3,2,1,0:T(8,128)(2,1)} copy(bf16[2,2,256,256]{3,2,1,0:T(8,128)(2,1)S(1)} %copy-done) | data formatting | bytes 1048576
  (2 shorter events, 0.0 us)
Async XLA Ops:
  0.6 0.7 %copy-start.3 = (bf16[1024]{0:T(1024)(128)(2,1)S(1)}, bf16[1024]{0:T(1024)(128)(2,1)}, u32[]{:S(2)}) copy-start(bf16[1024]{0:T(1024)(128)(2,1)} %param.9) | copy-start | bytes 6148
  1.3 0.7 %copy-start.4 = (bf16[1024]{0:T(1024)(128)(2,1)S(1)}, bf16[1024]{0:T(1024)(128)(2,1)}, u32[]{:S(2)}) copy-start(bf16[1024]{0:T(1024)(128)(2,1)} %param.10) | copy-start | bytes 6148
  2.0 0.7 %copy-start.2 = (s32[256,2]{0,1:T(2,128)S(1)}, s32[256,2]{0,1:T(2,128)}, u32[]{:S(2)}) copy-start(s32[256,2]{0,1:T(2,128)} %param.14) | copy-start | bytes 6148
  2.7 0.8 %copy-start.1 = (f32[350,2]{0,1:T(2,128)S(1)}, f32[350,2]{0,1:T(2,128)}, u32[]{:S(2)}) copy-start(f32[350,2]{0,1:T(2,128)} %param.13) | copy-start | bytes 8404
  46.1 1.9 %copy-start = (bf16[2,2,256,256]{3,2,1,0:T(8,128)(2,1)S(1)}, bf16[2,2,256,256]{3,2,1,0:T(8,128)(2,1)}, u32[]{:S(2)}) copy-start(bf16[2,2,256,256]{3,2,1,0:T(8,128)(2,1)} %get-tuple-element.5) | copy-start | bytes 1572868

commit v2 on v1

--- a/solution.py
+++ b/solution.py
@@ -25,6 +25,7 @@
 ROWS = 16
 GROUPS = 4
 CHUNKS = 4
+SLOTS = 3
 TILE = 256
 MESH = pl.DeviceIdType.MESH
 F32 = jnp.float32
@@ -47,9 +48,9 @@
 
 
 COS_FULL = fit_even(cos_turn, 0.5, 5)
-SIN_FULL = fit_even(sin_turn, 0.5, 5)
+SIN_FULL = fit_even(sin_turn, 0.5, 4)
 STEP_REACH = 0.12
-COS_STEP = fit_even(cos_turn, STEP_REACH, 3)
+COS_STEP = fit_even(cos_turn, STEP_REACH, 2)
 SIN_STEP = fit_even(sin_turn, STEP_REACH, 2)
 
 
@@ -58,6 +59,12 @@
     for c in coefs[-3::-1]:
         total = total * z + c
     return total
+
+
+def cos_minus_sin(turns):
+    r = turns - ((turns + ROUNDER) - ROUNDER)
+    z = r * r
+    return horner(COS_FULL, z), horner([-c for c in SIN_FULL], z) * r
 
 
 def sincos_turns(turns):
@@ -92,9 +99,11 @@
     n_freq, n_lst, chans, total_sources = dims
     local_src = scint_ref.shape[0]
     times = scint_ref.shape[1]
-    count = pairs_ref.shape[0]
+    count = pairs_ref.shape[1]
     group = count // GROUPS
     chips = n_freq // 2
+    blocks = local_src // SRC_BLOCK
+    tiles = total_sources // TILE
     part = local_src // CHUNKS
     me = lax.axis_index("freq")
     lst = lax.axis_index("lst")
@@ -137,25 +146,26 @@
     first_chan = (me * chans).astype(F32)
     nus = [NU_START + NU_STEP * (first_chan + c) for c in range(chans)]
 
-    antennas = coords_ref.shape[0]
-    ids = lax.broadcasted_iota(jnp.int32, (count, antennas), 1)
-    select = (pairs_ref[:, 0:1] == ids).astype(F32) - (pairs_ref[:, 1:2] == ids).astype(F32)
-    both = jnp.dot(select, coords_ref[...], precision=lax.Precision.HIGHEST, preferred_element_type=F32)
-    east, north = both[:, 0:1], both[:, 1:2]
-    lane = lax.broadcasted_iota(jnp.int32, (count, ROWS), 1)
+    antennas = coords_ref.shape[1]
+    ids = lax.broadcasted_iota(jnp.int32, (antennas, count), 0)
+    select = (pairs_ref[0:1, :] == ids).astype(F32) - (pairs_ref[1:2, :] == ids).astype(F32)
+    both = jnp.dot(coords_ref[...], select, precision=lax.Precision.HIGHEST, preferred_element_type=F32)
+    east = jnp.broadcast_to(both[0:1, :], (128, count)).T
+    north = jnp.broadcast_to(both[1:2, :], (128, count)).T
+    lane = lax.broadcasted_iota(jnp.int32, (count, 128), 1)
     pair_value = jnp.where(lane < 3, east, jnp.where(lane < 6, north, 0.0))
 
     def coef_rows(scale):
         high, middle, low = pieces(pair_value * scale)
         picked = jnp.where((lane == 0) | (lane == 3), high, jnp.where((lane == 1) | (lane == 4), middle, low))
-        return picked.astype(BF16)
+        return picked.astype(BF16)[:, :ROWS]
 
     main = coef_rows(nus[0] * (1.0 / C_LIGHT))
     step = coef_rows(NU_STEP / C_LIGHT)
     for g in range(GROUPS):
         coefs[g, 0:group, :] = main[g * group : (g + 1) * group]
         coefs[g, group : 2 * group, :] = step[g * group : (g + 1) * group]
-    lines[...] = jnp.broadcast_to(east, lines.shape)
+    lines[...] = east
 
     t_blocks = visible_ref.shape[0]
     spread = (
@@ -206,37 +216,51 @@
                 table = jnp.where(src_row == at, row, table)
             beam_rows[c, :, cols] = jnp.where(src_row < 10, table, 0.0).astype(BF16)
 
-    def trig(g):
-        @pl.loop(0, total_sources // TILE)
+    def trig_tile(g, i):
+        cols = pl.ds(pl.multiple_of(i * TILE, TILE), TILE)
+        turns = jnp.dot(coefs[g], phase_rows[:, cols], preferred_element_type=F32)
+        co, si = cos_minus_sin(turns[:group])
+        cd, sd = sincos_step(turns[group:])
+        for c in range(chans):
+            if c > 0:
+                co, si = co * cd + si * sd, si * cd - co * sd
+            planes[g % SLOTS, c, 0:group, cols] = co.astype(BF16)
+            planes[g % SLOTS, c, group : 2 * group, cols] = si.astype(BF16)
+
+    def trig(g, first, last):
+        @pl.loop(first, last)
         def _(i):
-            cols = pl.ds(pl.multiple_of(i * TILE, TILE), TILE)
-            turns = jnp.dot(coefs[g], phase_rows[:, cols], preferred_element_type=F32)
-            co, si = sincos_turns(turns[:group])
-            cd, sd = sincos_step(turns[group:])
-            for c in range(chans):
-                if c > 0:
-                    co, si = co * cd - si * sd, si * cd + co * sd
-                planes[g % 2, c, 0:group, cols] = co.astype(BF16)
-                planes[g % 2, c, group : 2 * group, cols] = (-si).astype(BF16)
+            trig_tile(g, i)
+
+    def amp_step(block, gains, k):
+        at = pl.multiple_of(block * local_src + k * SRC_BLOCK, SRC_BLOCK)
+        mask = mask_rows[pl.ds(block * blocks + k, 1), :]
+        gain = gains(pl.ds(pl.multiple_of(k * SRC_BLOCK, SRC_BLOCK), SRC_BLOCK)).astype(F32)
+        for c in range(chans):
+            right = jnp.where(row_id == 9, mask, beam_right[c]).astype(BF16)
+            power = rowdot(beam_rows[c, :, pl.ds(at, SRC_BLOCK)], right)
+            amps[c, pl.ds(at, SRC_BLOCK), :] = (jnp.exp2(power) * gain).astype(BF16)
+
+    def fused(g, first, per, block, gains):
+        @pl.loop(0, blocks)
+        def _(k):
+            amp_step(block, gains, k)
+            for q in range(per):
+                trig_tile(g, first + k * per + q)
 
     def amplitudes(block, gains):
-        @pl.loop(0, local_src // SRC_BLOCK)
+        @pl.loop(0, blocks // 2)
         def _(k):
-            at = pl.multiple_of(block * local_src + k * SRC_BLOCK, SRC_BLOCK)
-            mask = mask_rows[pl.ds(block * (local_src // SRC_BLOCK) + k, 1), :]
-            gain = gains(pl.ds(pl.multiple_of(k * SRC_BLOCK, SRC_BLOCK), SRC_BLOCK)).astype(F32)
-            for c in range(chans):
-                right = jnp.where(row_id == 9, mask, beam_right[c]).astype(BF16)
-                power = rowdot(beam_rows[c, :, pl.ds(at, SRC_BLOCK)], right)
-                amps[c, pl.ds(at, SRC_BLOCK), :] = (jnp.exp2(power) * gain).astype(BF16)
+            amp_step(block, gains, 2 * k)
+            amp_step(block, gains, 2 * k + 1)
 
     def multiply(g):
         rows = pl.ds(pl.multiple_of(g * group, group), group)
         for c in range(chans):
-            summed = jnp.dot(planes[g % 2, c], amps[c], preferred_element_type=F32)
+            summed = jnp.dot(planes[g % SLOTS, c], amps[c], preferred_element_type=F32)
             real, imag = summed[:group], summed[group:]
             scale = nus[c] * (OMEGA_STEP / C_LIGHT)
-            co, si = sincos_turns((lines[rows, :] * scale) * samples)
+            co, si = sincos_turns((lines[rows, 0:1] * scale) * samples)
             vis_ref[c, 0, rows, :] = (co * real + si * imag).astype(BF16)
             vis_ref[c, 1, rows, :] = (co * imag - si * real).astype(BF16)
 
@@ -263,18 +287,24 @@
             far_copies[k * (chips - 1) + d - 1].wait_recv()
             far(d, k).start()
 
-    trig(0)
+    per = min(2, tiles // blocks)
+    fused(0, 0, per, me, lambda rows: scint_ref[rows, :])
+    trig(0, per * blocks, tiles)
+    near_copy.wait()
     forward(0)
-    amplitudes(me, lambda rows: scint_ref[rows, :])
-    near_copy.wait()
     forward(1)
-    amplitudes(partner, lambda rows: gains_all[partner, rows, :])
-    trig(1)
-    for k in range(2, CHUNKS):
-        forward(k)
+    fused(1, 0, per, partner, lambda rows: gains_all[partner, rows, :])
+    trig(1, per * blocks, tiles)
+    forward(2)
+    trig(2, 0, tiles - blocks)
+    forward(3)
     for d in range(1, chips):
         src = ((chip + chips - d) % chips) * 2 + core
-        amplitudes(src, lambda rows, src=src: gains_all[src, rows, :])
+        gains = lambda rows, src=src: gains_all[src, rows, :]
+        if d == 1:
+            fused(2, tiles - blocks, 1, src, gains)
+        else:
+            amplitudes(src, gains)
     for k in range(CHUNKS):
         for d in range(1, chips):
             far(d, k).wait()
@@ -289,9 +319,9 @@
         multiply(g)
         send_group(g)
 
-        @pl.when(g + 2 < GROUPS)
+        @pl.when(g == GROUPS - 2)
         def _():
-            trig(g + 2)
+            trig(GROUPS - 1, 0, tiles)
 
     @pl.when(lst == 0)
     def _():
@@ -337,11 +367,11 @@
             pltpu.VMEM((n_freq, local_src, times), BF16),
             pltpu.VMEM((ROWS, total), BF16),
             pltpu.VMEM((chans, ROWS, total), BF16),
-            pltpu.VMEM((2, chans, 2 * group, total), BF16),
+            pltpu.VMEM((SLOTS, chans, 2 * group, total), BF16),
             pltpu.VMEM((chans, total, times), BF16),
             pltpu.VMEM((visible.shape[1], times), F32),
             pltpu.VMEM((GROUPS, 2 * group, ROWS), BF16),
-            pltpu.VMEM((count, times), F32),
+            pltpu.VMEM((count, 128), F32),
             pltpu.VMEM((chans, TAIL + times, times), BF16),
             pltpu.VMEM((8, TAIL + times), F32),
             pltpu.VMEM((chans, 2, count, TAIL), BF16),
@@ -354,7 +384,7 @@
         compiler_params=pltpu.CompilerParams(
             collective_id=0, has_side_effects=True, vmem_limit_bytes=64000000
         ),
-    )(sky, sky_scint, visible, antenna_coords, baseline_antennas, filter_taps)
+    )(sky, sky_scint, visible, antenna_coords.T, baseline_antennas.T, filter_taps)
 
 
 def solution(mesh):

time: 49 us -> 42.9 us (0.88)
  Pallas kernels: 41.7 us -> 36.6 us
  local copies, waits for them, and re-layouts: 5.77 us -> 4.76 us
    pallas_call x1, Pallas kernels: 41.7 us -> 36.6 us  [shards(): pl.pallas_call(functools.partial(kernel, (n_freq, n_lst, chans, total)),...]
    another operation x3, local copies, waits for them, and re-layouts: 0.7 us -> 0.01 us  [shards(): sky = jnp.stack([sky_east, sky_north, sky_flux, sky_flux]).astype(F32)]
    unnamed x14 -> x10, local copies, waits for them, and re-layouts: 5.07 us -> 4.75 us
where the time goes in v2:
time: 42.9 us; the launch traced here: 42.6 us
  Pallas kernels  36.6 us (85%)
  local copies, waits for them, and re-layouts  4.76 us (11%)
  between operations  0.66 us (2%)
  other arithmetic  0.63 us (1%)
    pallas_call x1, Pallas kernels, shards(): pl.pallas_call(functools.partial(kernel, (n_freq, n_lst, chans, total)),...  36.6 us
    unnamed x10, local copies, waits for them, and re-layouts  4.75 us

profile of v2, /device:TPU:0, one launch (start us, length us, event | category | flops | bytes accessed | tf_op | source)
XLA Modules:
  0.0 42.6 jit_solution(10809567110372183741)
XLA Ops:
  0.6 0.0 copy-start.1
  0.6 0.7 %copy-done.1 = bf16[1024]{0:T(1024)(128)(2,1)S(1)} copy-done((bf16[1024]{0:T(1024)(128)(2,1)S(1)}, bf16[1024]{0:T(1024)(128)(2,1)}, u32[]{:S(2)}) %copy-start.1) | copy-done | bytes 2072
  1.3 0.0 copy-start.2
  1.3 0.7 %copy-done.2 = bf16[1024]{0:T(1024)(128)(2,1)S(1)} copy-done((bf16[1024]{0:T(1024)(128)(2,1)S(1)}, bf16[1024]{0:T(1024)(128)(2,1)}, u32[]{:S(2)}) %copy-start.2) | copy-done | bytes 2072
  2.0 0.0 copy-start.3
  2.0 0.7 %copy-done.3 = bf16[1024]{0:T(1024)(128)(2,1)S(1)} copy-done((bf16[1024]{0:T(1024)(128)(2,1)S(1)}, bf16[1024]{0:T(1024)(128)(2,1)}, u32[]{:S(2)}) %copy-start.3) | copy-done | bytes 2072
  2.7 0.6 %maximum_convert_fusion.sky_ref = f32[4,1024]{1,0:T(4,128)} fusion(bf16[1,1024]{1,0:T(2,128)(2,1)S(1)} %stack.15, bf16[1,1024]{1,0:T(2,128)(2,1)S(1)} %stack.14, bf16[1,1024]{1,0:T(2,128)(2,1)S(1)} %stack.13), kind=kLoop, calls=%fused_computation | loop fusion | flops 32768 | bytes 22528 | tf_op jit(solution)/shard_map/convert_element_type | solution.py:355
  3.3 36.6 %shard_map.95 = (bf16[2,2,256,256]{3,2,1,0:T(8,128)(2,1)}, bf16[2,2,256,256]{3,2,1,0:T(8,128)(2,1)}) custom-call(f32[4,1024]{1,0:T(4,128)} %maximum_convert_fusion.sky_ref, bf16[1024,256]{1,0:T(8,128)(2,1)} %scint_ref.1, s32[32,32]{1,0:T(8,128)} %visible_ref.1, f32[2,350]{1,0:T(2,128)} %bitcast.2, s32[2,256]{1,0:T(2,128)} %bitcast.3, bf16[2,257]{1,0:T(2,128)(2,1)} %taps_ref.1), custom_call_target="tpu_custom_call" | custom-call | tf_op jit(solution)/shard_map/pallas_call | solution.py:360
  39.9 0.0 copy-start
  39.9 1.9 %copy.12 = bf16[2,2,256,256]{3,2,1,0:T(8,128)(2,1)} copy(bf16[2,2,256,256]{3,2,1,0:T(8,128)(2,1)} %get-tuple-element.4) | data formatting | bytes 1048576
  41.8 0.0 copy-done
  41.8 0.8 %copy.13 = bf16[2,2,256,256]{3,2,1,0:T(8,128)(2,1)} copy(bf16[2,2,256,256]{3,2,1,0:T(8,128)(2,1)S(1)} %copy-done) | data formatting | bytes 1048576
  (3 shorter events, 0.0 us)
Async XLA Ops:
  0.6 0.7 %copy-start.1 = (bf16[1024]{0:T(1024)(128)(2,1)S(1)}, bf16[1024]{0:T(1024)(128)(2,1)}, u32[]{:S(2)}) copy-start(bf16[1024]{0:T(1024)(128)(2,1)} %param.8) | copy-start | bytes 6148
  1.3 0.7 %copy-start.2 = (bf16[1024]{0:T(1024)(128)(2,1)S(1)}, bf16[1024]{0:T(1024)(128)(2,1)}, u32[]{:S(2)}) copy-start(bf16[1024]{0:T(1024)(128)(2,1)} %param.9) | copy-start | bytes 6148
  2.0 0.7 %copy-start.3 = (bf16[1024]{0:T(1024)(128)(2,1)S(1)}, bf16[1024]{0:T(1024)(128)(2,1)}, u32[]{:S(2)}) copy-start(bf16[1024]{0:T(1024)(128)(2,1)} %param.10) | copy-start | bytes 6148
  39.9 1.9 %copy-start = (bf16[2,2,256,256]{3,2,1,0:T(8,128)(2,1)S(1)}, bf16[2,2,256,256]{3,2,1,0:T(8,128)(2,1)}, u32[]{:S(2)}) copy-start(bf16[2,2,256,256]{3,2,1,0:T(8,128)(2,1)} %get-tuple-element.5) | copy-start | bytes 1572868

commit v3 on v2

--- a/solution.py
+++ b/solution.py
@@ -93,8 +93,8 @@
     dims,
     sky_ref, scint_ref, visible_ref, coords_ref, pairs_ref, taps_ref,
     vis_ref, out_ref,
-    sky_all, gains_all, phase_rows, beam_rows, planes, amps, mask_rows, coefs, lines, toep, tap_rows, tail,
-    sky_send, sky_recv, near_send, near_recv, far_send, far_recv, fwd_send, fwd_recv, halo_send, halo_recv,
+    sky_all, gains_all, phase_rows, beam_rows, planes, last_planes, amps, mask_rows, coefs, lines, toep, tap_rows, tail,
+    sky_send, sky_recv, near_send, near_recv, far_send, far_recv, fwd_send, fwd_recv, halo_send, halo_recv, own_sem,
 ):
     n_freq, n_lst, chans, total_sources = dims
     local_src = scint_ref.shape[0]
@@ -141,6 +141,8 @@
             far_copies.append(copy)
     near_copy = send(scint_ref, gains_all.at[me], near_send.at[0], near_recv.at[0], {"freq": partner})
     near_copy.start()
+    own_copy = pltpu.make_async_copy(scint_ref, gains_all.at[me], own_sem.at[0])
+    own_copy.start()
     sky_all[me] = sky_ref[...]
 
     first_chan = (me * chans).astype(F32)
@@ -217,6 +219,7 @@
             beam_rows[c, :, cols] = jnp.where(src_row < 10, table, 0.0).astype(BF16)
 
     def trig_tile(g, i):
+        store = last_planes if g == GROUPS - 1 else planes.at[g]
         cols = pl.ds(pl.multiple_of(i * TILE, TILE), TILE)
         turns = jnp.dot(coefs[g], phase_rows[:, cols], preferred_element_type=F32)
         co, si = cos_minus_sin(turns[:group])
@@ -224,8 +227,8 @@
         for c in range(chans):
             if c > 0:
                 co, si = co * cd + si * sd, si * cd - co * sd
-            planes[g % SLOTS, c, 0:group, cols] = co.astype(BF16)
-            planes[g % SLOTS, c, group : 2 * group, cols] = si.astype(BF16)
+            store[c, 0:group, cols] = co.astype(BF16)
+            store[c, group : 2 * group, cols] = si.astype(BF16)
 
     def trig(g, first, last):
         @pl.loop(first, last)
@@ -254,10 +257,10 @@
             amp_step(block, gains, 2 * k)
             amp_step(block, gains, 2 * k + 1)
 
-    def multiply(g):
+    def multiply(g, store):
         rows = pl.ds(pl.multiple_of(g * group, group), group)
         for c in range(chans):
-            summed = jnp.dot(planes[g % SLOTS, c], amps[c], preferred_element_type=F32)
+            summed = jnp.dot(store[c], amps[c], preferred_element_type=F32)
             real, imag = summed[:group], summed[group:]
             scale = nus[c] * (OMEGA_STEP / C_LIGHT)
             co, si = sincos_turns((lines[rows, 0:1] * scale) * samples)
@@ -288,7 +291,8 @@
             far(d, k).start()
 
     per = min(2, tiles // blocks)
-    fused(0, 0, per, me, lambda rows: scint_ref[rows, :])
+    own_copy.wait()
+    fused(0, 0, per, me, lambda rows: gains_all[me, rows, :])
     trig(0, per * blocks, tiles)
     near_copy.wait()
     forward(0)
@@ -301,10 +305,7 @@
     for d in range(1, chips):
         src = ((chip + chips - d) % chips) * 2 + core
         gains = lambda rows, src=src: gains_all[src, rows, :]
-        if d == 1:
-            fused(2, tiles - blocks, 1, src, gains)
-        else:
-            amplitudes(src, gains)
+        amplitudes(src, gains)
     for k in range(CHUNKS):
         for d in range(1, chips):
             far(d, k).wait()
@@ -314,14 +315,19 @@
     for copy in far_copies:
         copy.wait_send()
 
-    @pl.loop(0, GROUPS)
+    trig(2, tiles - blocks, tiles)
+    ahead = 5
+
+    @pl.loop(0, GROUPS - 1)
     def _(g):
-        multiply(g)
+        multiply(g, planes.at[g])
+        for q in range(ahead):
+            trig_tile(GROUPS - 1, g * ahead + q)
         send_group(g)
 
-        @pl.when(g == GROUPS - 2)
-        def _():
-            trig(GROUPS - 1, 0, tiles)
+    trig(GROUPS - 1, (GROUPS - 1) * ahead, tiles)
+    multiply(GROUPS - 1, last_planes)
+    send_group(GROUPS - 1)
 
     @pl.when(lst == 0)
     def _():
@@ -360,7 +366,7 @@
     return pl.pallas_call(
         functools.partial(kernel, (n_freq, n_lst, chans, total)),
         out_shape=(shape, shape),
-        in_specs=[vmem] * 6,
+        in_specs=[vmem, pl.BlockSpec(memory_space=pl.ANY)] + [vmem] * 4,
         out_specs=(vmem, vmem),
         scratch_shapes=[
             pltpu.VMEM((n_freq, 4, local_src), F32),
@@ -368,6 +374,7 @@
             pltpu.VMEM((ROWS, total), BF16),
             pltpu.VMEM((chans, ROWS, total), BF16),
             pltpu.VMEM((SLOTS, chans, 2 * group, total), BF16),
+            pltpu.VMEM((chans, 2 * group, total), BF16),
             pltpu.VMEM((chans, total, times), BF16),
             pltpu.VMEM((visible.shape[1], times), F32),
             pltpu.VMEM((GROUPS, 2 * group, ROWS), BF16),
@@ -379,10 +386,10 @@
             dma((1,)), dma((1,)),
             dma((far, CHUNKS)), dma((far, CHUNKS)),
             dma((far, CHUNKS)), dma((far, CHUNKS)),
-            dma((GROUPS,)), dma((GROUPS,)),
+            dma((GROUPS,)), dma((GROUPS,)), dma((1,)),
         ],
         compiler_params=pltpu.CompilerParams(
-            collective_id=0, has_side_effects=True, vmem_limit_bytes=64000000
+            collective_id=0, has_side_effects=True, vmem_limit_bytes=66000000
         ),
     )(sky, sky_scint, visible, antenna_coords.T, baseline_antennas.T, filter_taps)
 

time: 42.9 us -> 44.8 us (1.044)
  Pallas kernels: 36.6 us -> 38.5 us
    pallas_call x1, Pallas kernels: 36.6 us -> 38.5 us  [shards(): pl.pallas_call(functools.partial(kernel, (n_freq, n_lst, chans, total)),...]
where the time goes in v3:
time: 44.8 us; the launch traced here: 44.6 us
  Pallas kernels  38.5 us (86%)
  local copies, waits for them, and re-layouts  4.76 us (11%)
  between operations  0.66 us (1%)
  other arithmetic  0.63 us (1%)
    pallas_call x1, Pallas kernels, shards(): pl.pallas_call(functools.partial(kernel, (n_freq, n_lst, chans, total)),...  38.5 us
    unnamed x10, local copies, waits for them, and re-layouts  4.75 us

profile of v3, /device:TPU:0, one launch (start us, length us, event | category | flops | bytes accessed | tf_op | source)
XLA Modules:
  0.0 44.6 jit_solution(9685239943064367949)
XLA Ops:
  0.6 0.0 copy-start.1
  0.6 0.7 %copy-done.1 = bf16[1024]{0:T(1024)(128)(2,1)S(1)} copy-done((bf16[1024]{0:T(1024)(128)(2,1)S(1)}, bf16[1024]{0:T(1024)(128)(2,1)}, u32[]{:S(2)}) %copy-start.1) | copy-done | bytes 2072
  1.3 0.0 copy-start.2
  1.3 0.7 %copy-done.2 = bf16[1024]{0:T(1024)(128)(2,1)S(1)} copy-done((bf16[1024]{0:T(1024)(128)(2,1)S(1)}, bf16[1024]{0:T(1024)(128)(2,1)}, u32[]{:S(2)}) %copy-start.2) | copy-done | bytes 2072
  2.0 0.0 copy-start.3
  2.0 0.7 %copy-done.3 = bf16[1024]{0:T(1024)(128)(2,1)S(1)} copy-done((bf16[1024]{0:T(1024)(128)(2,1)S(1)}, bf16[1024]{0:T(1024)(128)(2,1)}, u32[]{:S(2)}) %copy-start.3) | copy-done | bytes 2072
  2.7 0.6 %maximum_convert_fusion.sky_ref = f32[4,1024]{1,0:T(4,128)} fusion(bf16[1,1024]{1,0:T(2,128)(2,1)S(1)} %stack.15, bf16[1,1024]{1,0:T(2,128)(2,1)S(1)} %stack.14, bf16[1,1024]{1,0:T(2,128)(2,1)S(1)} %stack.13), kind=kLoop, calls=%fused_computation | loop fusion | flops 32768 | bytes 22528 | tf_op jit(solution)/shard_map/convert_element_type | solution.py:361
  3.3 38.5 %shard_map.95 = (bf16[2,2,256,256]{3,2,1,0:T(8,128)(2,1)}, bf16[2,2,256,256]{3,2,1,0:T(8,128)(2,1)}) custom-call(f32[4,1024]{1,0:T(4,128)} %maximum_convert_fusion.sky_ref, bf16[1024,256]{1,0:T(8,128)(2,1)} %scint_ref.1, s32[32,32]{1,0:T(8,128)} %visible_ref.1, f32[2,350]{1,0:T(2,128)} %bitcast.2, s32[2,256]{1,0:T(2,128)} %bitcast.3, bf16[2,257]{1,0:T(2,128)(2,1)} %taps_ref.1), custom_call_target="tpu_custom_call" | custom-call | tf_op jit(solution)/shard_map/pallas_call | solution.py:366
  41.8 0.0 copy-start
  41.8 1.9 %copy.12 = bf16[2,2,256,256]{3,2,1,0:T(8,128)(2,1)} copy(bf16[2,2,256,256]{3,2,1,0:T(8,128)(2,1)} %get-tuple-element.4) | data formatting | bytes 1048576
  43.8 0.0 copy-done
  43.8 0.8 %copy.13 = bf16[2,2,256,256]{3,2,1,0:T(8,128)(2,1)} copy(bf16[2,2,256,256]{3,2,1,0:T(8,128)(2,1)S(1)} %copy-done) | data formatting | bytes 1048576
  (3 shorter events, 0.0 us)
Async XLA Ops:
  0.6 0.7 %copy-start.1 = (bf16[1024]{0:T(1024)(128)(2,1)S(1)}, bf16[1024]{0:T(1024)(128)(2,1)}, u32[]{:S(2)}) copy-start(bf16[1024]{0:T(1024)(128)(2,1)} %param.8) | copy-start | bytes 6148
  1.3 0.7 %copy-start.2 = (bf16[1024]{0:T(1024)(128)(2,1)S(1)}, bf16[1024]{0:T(1024)(128)(2,1)}, u32[]{:S(2)}) copy-start(bf16[1024]{0:T(1024)(128)(2,1)} %param.9) | copy-start | bytes 6148
  2.0 0.7 %copy-start.3 = (bf16[1024]{0:T(1024)(128)(2,1)S(1)}, bf16[1024]{0:T(1024)(128)(2,1)}, u32[]{:S(2)}) copy-start(bf16[1024]{0:T(1024)(128)(2,1)} %param.10) | copy-start | bytes 6148
  41.8 1.9 %copy-start = (bf16[2,2,256,256]{3,2,1,0:T(8,128)(2,1)S(1)}, bf16[2,2,256,256]{3,2,1,0:T(8,128)(2,1)}, u32[]{:S(2)}) copy-start(bf16[2,2,256,256]{3,2,1,0:T(8,128)(2,1)} %get-tuple-element.5) | copy-start | bytes 1572868
